TPU v7x, 256 devices: a whole 4x4x8 slice. The times are simulated.
256 devices in a mesh: atoms: 4 (over y), frames: 64 (over x, z, core).
Axes of the slice: x: 4, y: 4, z: 8, core: 2. Of those that a mesh axis runs over, the one named last changes fastest.
Arguments:
- frames: float32 [1536, 3, 98304], P('frames', None, 'atoms'), may hold values from -48 to 48
- mean_structure: float32 [3, 98304], P(None, 'atoms'), may hold values from -16 to 16
- atom_weight: float32 [98304], P('atoms'), may hold values from 1 to 32
- subspace: bfloat16 [32, 3, 98304], P(None, None, 'atoms'), may hold values from -6 to 6
Outputs:
- new_mean: float32 [3, 98304], P(None, ('atoms', 'frames'))
- image: float32 [32, 3, 98304], P(None, None, ('atoms', 'frames'))
- basis: float32 [32, 3, 98304], P(None, None, ('atoms', 'frames'))
All inputs are finite; a program needn't handle non-finite values.
Results may differ from a plain program's by a relative error of at most 0.0076.
Values may be sent and summed in bfloat16 or wider, within the bound.
A program may use at most 128 MiB of HBM per device.

v0:
```python
import jax
import jax.numpy as jnp
from jax import lax
from jax.sharding import PartitionSpec as P

A = 98304
NEWTON = 8


def newton_polar(moment):
    norm = jnp.sqrt(jnp.sum(moment * moment, axis=(1, 2)))
    x = moment / norm[:, None, None]
    for step in range(NEWTON):
        x00, x01, x02 = (x[:, 0, 0], x[:, 0, 1], x[:, 0, 2])
        x10, x11, x12 = (x[:, 1, 0], x[:, 1, 1], x[:, 1, 2])
        x20, x21, x22 = (x[:, 2, 0], x[:, 2, 1], x[:, 2, 2])
        c00 = x11 * x22 - x12 * x21
        c01 = x12 * x20 - x10 * x22
        c02 = x10 * x21 - x11 * x20
        c10 = x02 * x21 - x01 * x22
        c11 = x00 * x22 - x02 * x20
        c12 = x01 * x20 - x00 * x21
        c20 = x01 * x12 - x02 * x11
        c21 = x02 * x10 - x00 * x12
        c22 = x00 * x11 - x01 * x10
        determ = x00 * c00 + x01 * c01 + x02 * c02
        cofac = jnp.stack(
            [
                jnp.stack([c00, c01, c02], axis=1),
                jnp.stack([c10, c11, c12], axis=1),
                jnp.stack([c20, c21, c22], axis=1),
            ],
            axis=1,
        )
        x = 0.5 * (x + cofac / determ[:, None, None])
    return x


def per_device(frames, mean_structure, atom_weight, subspace):
    highest = lax.Precision.HIGHEST
    frame_count = frames.shape[0] * lax.axis_size("frames")
    weighted = atom_weight[None, :] * mean_structure
    local_first = jnp.einsum("a,fia->fi", atom_weight, frames, precision=highest)
    total, mean_sum = lax.psum((jnp.sum(atom_weight), jnp.sum(weighted, axis=1)), "atoms")
    mean_center = mean_sum / total
    centered = (mean_structure - mean_center[:, None]) * atom_weight[None, :]
    local_second = jnp.einsum("ia,fja->fij", centered, frames, precision=highest)
    first, second = lax.psum((local_first, local_second), "atoms")
    moment = second / total
    frame_center = first / total
    rotation = newton_polar(moment)
    anchor = mean_center[:, None] - mean_structure
    moved = jnp.einsum("fij,fja->fia", rotation, frames, precision=highest)
    offset = jnp.einsum("fij,fj->fi", rotation, frame_center, precision=highest)
    displaced = (moved - offset[:, :, None] + anchor[None]).astype(jnp.bfloat16)
    frame_rows = displaced.shape[0]
    vectors = subspace.shape[0]
    local_proj = jnp.einsum(
        "fc,kc->fk",
        displaced.reshape(frame_rows, -1),
        subspace.reshape(vectors, -1),
        preferred_element_type=jnp.float32,
    )
    projection = lax.psum(local_proj, "atoms")
    proj_total = lax.psum(jnp.sum(local_proj, axis=0), ("atoms", "frames"))
    centered_projection = (projection - proj_total / frame_count).astype(jnp.bfloat16)
    term = jnp.einsum(
        "fk,fia->kia", centered_projection, displaced, preferred_element_type=jnp.float32
    )
    shift_sum = jnp.sum(displaced, axis=0, dtype=jnp.float32)
    stacked = jnp.concatenate([term, shift_sum[None]], axis=0)
    reduced = lax.psum_scatter(stacked, "frames", scatter_dimension=2, tiled=True)
    image_sum = reduced[:vectors]
    mean_shift = reduced[vectors]
    image = image_sum / frame_count
    width = image.shape[2]
    own_mean = lax.dynamic_slice_in_dim(mean_structure, lax.axis_index("frames") * width, width, 1)
    new_mean = own_mean + mean_shift / frame_count
    flat = image.reshape(vectors, -1)
    gram = lax.psum(jnp.dot(flat, flat.T, precision=highest), ("atoms", "frames")) / (3 * A)
    lower = jnp.linalg.cholesky(gram)
    basis = jax.scipy.linalg.solve_triangular(lower, flat, lower=True)
    return (new_mean, image, basis.reshape(image.shape))


def solution(mesh):
    return jax.shard_map(
        per_device,
        mesh=mesh,
        in_specs=(P("frames", None, "atoms"), P(None, "atoms"), P("atoms"), P(None, None, "atoms")),
        out_specs=(
            P(None, ("atoms", "frames")),
            P(None, None, ("atoms", "frames")),
            P(None, None, ("atoms", "frames")),
        ),
        check_vma=False,
    )
```

profile of v0, /device:TPU:1, one launch (start us, length us, event | category | flops | bytes accessed | tf_op | source)
XLA Modules:
  0.0 459.7 jit_solution(17343104478468763775)
XLA Ops:
  7.2 1.3 multiply_reduce_fusion
  8.6 1.5 reduce_sum.46
  10.1 10.1 %all-reduce.1 = (f32[3]{0:T(128)S(1)}, f32[]{:T(128)}) all-reduce(f32[3]{0:T(128)S(1)} %multiply_reduce_fusion, f32[]{:T(128)} %reduce_sum.46), channel_id=1, replica_groups=mesh['atoms'=4,'frames'=64] {'atoms'}, use_global_device_ids=true, to_apply=%region_1.0 | all-reduce | flops 4 | bytes 32 | tf_op jit(solution)/shard_map/psum | solution.py:44
  20.2 0.8 broadcast_divide_fusion.2
  21.0 16.9 %convolution_bitcast_fusion.1 = f32[24,3,3]{0,1,2:T(4,128)S(1)} fusion(f32[24,3,24576]{2,0,1:T(8,128)} %param.4, f32[3,24576]{1,0:T(4,128)} %param.5, f32[3]{0:T(128)S(1)} %broadcast_divide_fusion.2, f32[24576]{0:T(1024)} %param.6), kind=kOutput, calls=%fused_computation.12 | convolution fusion | flops 63848448 | bytes 7471980 | tf_op jit(solution)/shard_map/ia,fja->fij/dot_general | solution.py:47
  38.0 13.8 %fusion.34 = f32[1,24,3]{1,0,2:T(1,128)S(1)} fusion(f32[24576,1,1]{0,1,2:T(1,128)S(1)} %bitcast.242, f32[24,3,24576]{2,0,1:T(8,128)S(1)} %copy-done), kind=kOutput, calls=%fused_computation.168 | convolution fusion | flops 21233664 | bytes 7176480 | tf_op jit(solution)/shard_map/a,fia->fi/dot_general | solution.py:43
  51.8 11.1 %all-reduce = (f32[24,3,3]{0,1,2:T(4,128)S(1)}, f32[24,3]{1,0:T(8,128)S(1)}) all-reduce(f32[24,3,3]{0,1,2:T(4,128)S(1)} %convolution_bitcast_fusion.1, f32[24,3]{1,0:T(8,128)S(1)} %bitcast.243), channel_id=1, replica_groups=mesh['atoms'=4,'frames'=64] {'atoms'}, use_global_device_ids=true, to_apply=%region_4.0 | all-reduce | flops 288 | bytes 2304 | tf_op jit(solution)/shard_map/psum | solution.py:48
  62.9 0.7 fusion.32
  63.6 0.7 sqrt_multiply_fusion
  65.9 0.7 broadcast_divide_fusion
  66.9 29.3 %convert_reduce_fusion = (f32[3,24576]{1,0:T(4,128)S(1)}, bf16[24,3,24576]{2,1,0:T(4,128)(2,1)S(1)}) fusion(f32[3,24576]{1,0:T(4,128)S(1)} %broadcast_subtract_fusion, f32[24,3]{1,0:T(8,128)S(1)} %bitcast.269, f32[24,3,3]{2,1,0:T(4,128)S(1)} %copy.62, f32[24,3,24576]{2,0,1:T(8,128)} %param.4), kind=kOutput, calls=%fused_computation.5 | convolution fusion | flops 72474624 | bytes 11207808 | tf_op jit(solution)/shard_map/fij,fja->fia/dot_general | solution.py:53
  96.2 2.1 copy-done.1
  98.3 5.1 %fusion.33 = (f32[32]{0:T(128)S(1)}, f32[24,32]{1,0:T(8,128)S(1)}) fusion(bf16[32,3,24576]{2,0,1:T(8,128)(2,1)S(1)} %bitcast.241, bf16[24,3,24576]{2,1,0:T(4,128)(2,1)S(1)} %get-tuple-element.88), kind=kOutput, calls=%fused_computation.166 | convolution fusion | flops 113246944 | bytes 8260736 | tf_op jit(solution)/shard_map/fc,kc->fk/dot_general | solution.py:58
  103.5 12.2 %psum.53 = f32[24,32]{1,0:T(8,128)S(1)} all-reduce(f32[24,32]{1,0:T(8,128)S(1)} %get-tuple-element.90), channel_id=1, replica_groups=mesh['atoms'=4,'frames'=64] {'atoms'}, use_global_device_ids=true, to_apply=%region_7.0 | all-reduce | flops 768 | bytes 6144 | tf_op jit(solution)/shard_map/psum | solution.py:64
  115.7 87.8 %psum.54 = f32[32]{0:T(128)S(1)} all-reduce(f32[32]{0:T(128)S(1)} %get-tuple-element.89), channel_id=1, replica_groups=mesh['atoms'=4,'frames'=64] {'atoms','frames'}, use_global_device_ids=true, to_apply=%region_9.0 | all-reduce | flops 32 | bytes 256 | tf_op jit(solution)/shard_map/psum | solution.py:65
  203.6 9.0 %fusion.3 = f32[32,3,24576]{2,0,1:T(8,128)S(1)} fusion(bf16[24,3,24576]{2,1,0:T(4,128)(2,1)} %copy-done.1, f32[24,32]{1,0:T(8,128)S(1)} %psum.53, f32[32]{0:T(128)S(1)} %broadcast_multiply_fusion.1), kind=kOutput, calls=%fused_computation.6 | convolution fusion | flops 113247744 | bytes 12979328 | tf_op jit(solution)/shard_map/fk,fia->kia/dot_general | solution.py:67
  212.6 5.7 %pad_maximum_fusion = f32[33,3,24576]{2,0,1:T(8,128)} fusion(f32[1,3,24576]{2,0,1:T(1,128)S(1)} %broadcast_in_dim.3, f32[32,3,24576]{2,0,1:T(8,128)S(1)} %fusion.3), kind=kLoop, calls=%fused_computation.3 | loop fusion | flops 2433024 | bytes 19464192 | tf_op jit(solution)/shard_map/concatenate | solution.py:71
  218.3 144.5 %reduce-scatter.2.cloned.1.call-done = f32[33,3,384]{2,0,1:T(8,128)} async-done(((f32[33,3,24576]{2,0,1:T(8,128)}), f32[33,3,384]{2,0,1:T(8,128)}) %reduce-scatter.2.cloned.1.call-update) | async-done | bytes 152080 | tf_op jit(solution)/shard_map/reduce_scatter | solution.py:72
  362.8 0.9 slice_multiply_fusion
  364.0 78.6 %psum.55 = f32[32,32]{0,1:T(8,128)S(1)} all-reduce(f32[32,32]{0,1:T(8,128)S(1)} %convolution_bitcast_fusion), channel_id=1, replica_groups=mesh['atoms'=4,'frames'=64] {'atoms','frames'}, use_global_device_ids=true, to_apply=%region_12.0 | all-reduce | flops 1024 | bytes 8192 | tf_op jit(solution)/shard_map/psum | solution.py:80
  442.7 2.9 cholesky.16
  446.9 2.4 custom-call.7
  449.4 0.8 slice_multiply_fusion.1
  450.8 1.9 fusion.15
  (102 shorter events, 4.1 us)
Async XLA Ops:
  7.2 30.8 %copy-start.3 = (f32[24576]{0:T(1024)S(1)}, f32[24576]{0:T(1024)}, u32[]{:S(2)}) copy-start(f32[24576]{0:T(1024)} %param.6) | copy-start | bytes 294916
  7.2 355.6 %reduce-scatter.2.cloned.1.call-start = ((), (), s32[]{:S(2)}) async-start(), calls=%async_computation.1 | async-start | bytes 11980800 | tf_op jit(solution)/shard_map/reduce_scatter | solution.py:72
  20.2 17.7 %copy-start = (f32[24,3,24576]{2,0,1:T(8,128)S(1)}, f32[24,3,24576]{2,0,1:T(8,128)}, u32[]{:S(2)}) copy-start(f32[24,3,24576]{2,0,1:T(8,128)} %param.4) | copy-start | bytes 21233668
  21.0 44.4 %copy-start.2 = (f32[3,24576]{1,0:T(4,128)S(1)}, f32[3,24576]{1,0:T(4,128)}, u32[]{:S(2)}) copy-start(f32[3,24576]{1,0:T(4,128)} %param.5) | copy-start | bytes 884740
  65.5 32.9 %slice-start = ((s8[4718592]{0:T(1024)(128)(4,1)}), s8[524288]{0:T(1024)(128)(4,1)S(1)}, s32[]{:S(2)}) async-start(s8[4718592]{0:T(1024)(128)(4,1)} %bitcast.240), calls=%async_computation.2 | async-start | bytes 1048576
  66.9 31.5 %slice-start.1 = ((s8[4718592]{0:T(1024)(128)(4,1)}), s8[4194304]{0:T(1024)(128)(4,1)S(1)}, s32[]{:S(2)}) async-start(s8[4718592]{0:T(1024)(128)(4,1)} %bitcast.240), calls=%async_computation.3 | async-start | bytes 8388608
  96.2 2.1 copy-start.1
  363.7 89.0 %copy-start.4 = (f32[32,3,384]{2,0,1:T(8,128)}, f32[32,3,384]{2,0,1:T(8,128)S(1)}, u32[]{:S(2)}) copy-start(f32[32,3,384]{2,0,1:T(8,128)S(1)} %slice_multiply_fusion) | copy-start | bytes 442372
Sparse Core Ops, SparseCore 0:
  218.4 144.3 reduce-scatter.1
where the time goes:
time: 464 us; the launch traced here: 460 us
  blocking collectives  200 us (43%)
  waiting for transfers between devices  144 us (31%)
  matrix products  76.6 us (17%)
  other arithmetic  21.2 us (5%)
  between operations  14.9 us (3%)
    reduce_scatter x1, waiting for transfers between devices, per_device(): lax.psum_scatter(stacked, 'frames', scatter_dimension=2, tiled=True)  144 us
    psum x1, blocking collectives, per_device(): proj_total = lax.psum(jnp.sum(local_proj, axis=0), ('atoms', 'frames'))  87.8 us
    psum x1, blocking collectives, per_device(): lax.psum(jnp.dot(flat, flat.T, precision=highest), ('atoms', 'frames'))  78.6 us
    dot_general x1, matrix products, per_device(): moved = jnp.einsum('fij,fja->fia', rotation, frames, precision=highest)  29.3 us
    dot_general x1, matrix products, per_device(): jnp.einsum('ia,fja->fij', centered, frames, precision=highest)  16.9 us
    dot_general x1, matrix products, per_device(): jnp.einsum('a,fia->fi', atom_weight, frames, precision=highest)  13.8 us
    psum x1, blocking collectives, per_device(): projection = lax.psum(local_proj, 'atoms')  12.2 us
    psum x1, blocking collectives, per_device(): first, second = lax.psum((local_first, local_second), 'atoms')  11.1 us
  transfers between devices with their start and end apart: 1, of which 1 were waited for; matrix products, arithmetic and copies ran while one was open for 0% of the time, Pallas kernels for 0%

commit v1 on v0

--- a/solution.py
+++ b/solution.py
@@ -77,7 +77,7 @@
     own_mean = lax.dynamic_slice_in_dim(mean_structure, lax.axis_index("frames") * width, width, 1)
     new_mean = own_mean + mean_shift / frame_count
     flat = image.reshape(vectors, -1)
-    gram = lax.psum(jnp.dot(flat, flat.T, precision=highest), ("atoms", "frames")) / (3 * A)
+    gram = lax.psum(lax.psum(jnp.dot(flat, flat.T, precision=highest), "frames"), "atoms") / (3 * A)
     lower = jnp.linalg.cholesky(gram)
     basis = jax.scipy.linalg.solve_triangular(lower, flat, lower=True)
     return (new_mean, image, basis.reshape(image.shape))

time: 464 us -> 650 us (1.40)
  blocking collectives: 200 us -> 380 us
    psum x1 -> x2, blocking collectives: 78.6 us -> 259 us  [the longest x1 245 us: per_device(): lax.psum(jnp.dot(flat, flat.T, precision=highest), 'frames')]
where the time goes in v1:
time: 650 us; the launch traced here: 640 us
  blocking collectives  380 us (58%)
  waiting for transfers between devices  145 us (22%)
  matrix products  76.3 us (12%)
  other arithmetic  21.2 us (3%)
  between operations  14.9 us (2%)
    psum x1, blocking collectives, per_device(): lax.psum(jnp.dot(flat, flat.T, precision=highest), 'frames')  245 us
    reduce_scatter x1, waiting for transfers between devices, per_device(): lax.psum_scatter(stacked, 'frames', scatter_dimension=2, tiled=True)  144 us
    psum x1, blocking collectives, per_device(): proj_total = lax.psum(jnp.sum(local_proj, axis=0), ('atoms', 'frames'))  87.7 us
    dot_general x1, matrix products, per_device(): moved = jnp.einsum('fij,fja->fia', rotation, frames, precision=highest)  29.3 us
    dot_general x1, matrix products, per_device(): jnp.einsum('ia,fja->fij', centered, frames, precision=highest)  16.7 us
    dot_general x1, matrix products, per_device(): jnp.einsum('a,fia->fi', atom_weight, frames, precision=highest)  13.8 us
    psum x1, blocking collectives, per_device(): lax.psum(lax.psum(jnp.dot(flat, flat.T, precision=highest), 'frames'), 'a...  13.4 us
  transfers between devices with their start and end apart: 1, of which 1 were waited for; matrix products, arithmetic and copies ran while one was open for 0% of the time, Pallas kernels for 0%

profile of v1, /device:TPU:1, one launch (start us, length us, event | category | flops | bytes accessed | tf_op | source)
XLA Modules:
  0.0 639.7 jit_solution(10879651342355483180)
XLA Ops:
  7.2 1.3 multiply_reduce_fusion
  8.6 1.5 reduce_sum.46
  10.1 10.1 %all-reduce.1 = (f32[3]{0:T(128)S(1)}, f32[]{:T(128)}) all-reduce(f32[3]{0:T(128)S(1)} %multiply_reduce_fusion, f32[]{:T(128)} %reduce_sum.46), channel_id=1, replica_groups=mesh['atoms'=4,'frames'=64] {'atoms'}, use_global_device_ids=true, to_apply=%region_1.0 | all-reduce | flops 4 | bytes 32 | tf_op jit(solution)/shard_map/psum | solution.py:44
  20.2 0.8 broadcast_divide_fusion.2
  21.0 16.7 %convolution_bitcast_fusion.1 = f32[24,3,3]{0,1,2:T(4,128)S(1)} fusion(f32[24,3,24576]{2,0,1:T(8,128)} %param.4, f32[3,24576]{1,0:T(4,128)} %param.5, f32[3]{0:T(128)S(1)} %broadcast_divide_fusion.2, f32[24576]{0:T(1024)} %param.6), kind=kOutput, calls=%fused_computation.12 | convolution fusion | flops 63848448 | bytes 7471980 | tf_op jit(solution)/shard_map/ia,fja->fij/dot_general | solution.py:47
  37.8 13.8 %fusion.34 = f32[1,24,3]{1,0,2:T(1,128)S(1)} fusion(f32[24576,1,1]{0,1,2:T(1,128)S(1)} %bitcast.242, f32[24,3,24576]{2,0,1:T(8,128)S(1)} %copy-done), kind=kOutput, calls=%fused_computation.168 | convolution fusion | flops 21233664 | bytes 7176480 | tf_op jit(solution)/shard_map/a,fia->fi/dot_general | solution.py:43
  51.6 11.4 %all-reduce = (f32[24,3,3]{0,1,2:T(4,128)S(1)}, f32[24,3]{1,0:T(8,128)S(1)}) all-reduce(f32[24,3,3]{0,1,2:T(4,128)S(1)} %convolution_bitcast_fusion.1, f32[24,3]{1,0:T(8,128)S(1)} %bitcast.243), channel_id=1, replica_groups=mesh['atoms'=4,'frames'=64] {'atoms'}, use_global_device_ids=true, to_apply=%region_4.0 | all-reduce | flops 288 | bytes 2304 | tf_op jit(solution)/shard_map/psum | solution.py:48
  63.0 0.7 fusion.32
  63.7 0.7 sqrt_multiply_fusion
  67.0 29.3 %convert_reduce_fusion = (f32[3,24576]{1,0:T(4,128)S(1)}, bf16[24,3,24576]{2,1,0:T(4,128)(2,1)S(1)}) fusion(f32[3,24576]{1,0:T(4,128)S(1)} %broadcast_subtract_fusion, f32[24,3]{1,0:T(8,128)S(1)} %bitcast.269, f32[24,3,3]{2,1,0:T(4,128)S(1)} %copy.62, f32[24,3,24576]{2,0,1:T(8,128)} %param.4), kind=kOutput, calls=%fused_computation.5 | convolution fusion | flops 72474624 | bytes 11207808 | tf_op jit(solution)/shard_map/fij,fja->fia/dot_general | solution.py:53
  96.3 2.1 copy-done.1
  98.4 5.1 fusion.33
  103.5 12.2 %psum.60 = f32[24,32]{1,0:T(8,128)S(1)} all-reduce(f32[24,32]{1,0:T(8,128)S(1)} %get-tuple-element.90), channel_id=1, replica_groups=mesh['atoms'=4,'frames'=64] {'atoms'}, use_global_device_ids=true, to_apply=%region_7.0 | all-reduce | flops 768 | bytes 6144 | tf_op jit(solution)/shard_map/psum | solution.py:64
  115.7 87.7 %psum.61 = f32[32]{0:T(128)S(1)} all-reduce(f32[32]{0:T(128)S(1)} %get-tuple-element.89), channel_id=1, replica_groups=mesh['atoms'=4,'frames'=64] {'atoms','frames'}, use_global_device_ids=true, to_apply=%region_9.0 | all-reduce | flops 32 | bytes 256 | tf_op jit(solution)/shard_map/psum | solution.py:65
  203.7 9.0 %fusion.3 = f32[32,3,24576]{2,0,1:T(8,128)S(1)} fusion(bf16[24,3,24576]{2,1,0:T(4,128)(2,1)} %copy-done.1, f32[24,32]{1,0:T(8,128)S(1)} %psum.60, f32[32]{0:T(128)S(1)} %broadcast_multiply_fusion.1), kind=kOutput, calls=%fused_computation.6 | convolution fusion | flops 113247744 | bytes 12979328 | tf_op jit(solution)/shard_map/fk,fia->kia/dot_general | solution.py:67
  212.6 5.7 pad_maximum_fusion
  218.3 144.5 %reduce-scatter.2.cloned.1.call-done = f32[33,3,384]{2,0,1:T(8,128)} async-done(((f32[33,3,24576]{2,0,1:T(8,128)}), f32[33,3,384]{2,0,1:T(8,128)}) %reduce-scatter.2.cloned.1.call-update) | async-done | bytes 152080 | tf_op jit(solution)/shard_map/reduce_scatter | solution.py:72
  362.8 0.9 slice_multiply_fusion
  364.0 245.2 %psum.62 = f32[32,32]{0,1:T(8,128)S(1)} all-reduce(f32[32,32]{0,1:T(8,128)S(1)} %convolution_bitcast_fusion), channel_id=1, replica_groups=mesh['atoms'=4,'frames'=64] {'frames'}, use_global_device_ids=true, to_apply=%region_12.0 | all-reduce | flops 1024 | bytes 8192 | tf_op jit(solution)/shard_map/psum | solution.py:80
  609.2 13.4 %psum.63 = f32[32,32]{0,1:T(8,128)S(1)} all-reduce(f32[32,32]{0,1:T(8,128)S(1)} %psum.62), channel_id=1, replica_groups=mesh['atoms'=4,'frames'=64] {'atoms'}, use_global_device_ids=true, to_apply=%region_13.0 | all-reduce | flops 1024 | bytes 8192 | tf_op jit(solution)/shard_map/psum | solution.py:80
  622.7 2.9 cholesky.16
  627.0 2.4 custom-call.7
  629.4 0.8 slice_multiply_fusion.1
  630.8 1.9 fusion.15
  (103 shorter events, 4.7 us)
Async XLA Ops:
  7.2 30.6 %copy-start.3 = (f32[24576]{0:T(1024)S(1)}, f32[24576]{0:T(1024)}, u32[]{:S(2)}) copy-start(f32[24576]{0:T(1024)} %param.6) | copy-start | bytes 294916
  7.2 355.7 %reduce-scatter.2.cloned.1.call-start = ((), (), s32[]{:S(2)}) async-start(), calls=%async_computation.1 | async-start | bytes 11980800 | tf_op jit(solution)/shard_map/reduce_scatter | solution.py:72
  20.2 17.5 %copy-start = (f32[24,3,24576]{2,0,1:T(8,128)S(1)}, f32[24,3,24576]{2,0,1:T(8,128)}, u32[]{:S(2)}) copy-start(f32[24,3,24576]{2,0,1:T(8,128)} %param.4) | copy-start | bytes 21233668
  21.0 44.5 %copy-start.2 = (f32[3,24576]{1,0:T(4,128)S(1)}, f32[3,24576]{1,0:T(4,128)}, u32[]{:S(2)}) copy-start(f32[3,24576]{1,0:T(4,128)} %param.5) | copy-start | bytes 884740
  65.6 32.8 %slice-start = ((s8[4718592]{0:T(1024)(128)(4,1)}), s8[524288]{0:T(1024)(128)(4,1)S(1)}, s32[]{:S(2)}) async-start(s8[4718592]{0:T(1024)(128)(4,1)} %bitcast.240), calls=%async_computation.2 | async-start | bytes 1048576
  66.9 31.4 %slice-start.1 = ((s8[4718592]{0:T(1024)(128)(4,1)}), s8[4194304]{0:T(1024)(128)(4,1)S(1)}, s32[]{:S(2)}) async-start(s8[4718592]{0:T(1024)(128)(4,1)} %bitcast.240), calls=%async_computation.3 | async-start | bytes 8388608
  96.2 2.1 copy-start.1
  363.8 269.0 %copy-start.4 = (f32[32,3,384]{2,0,1:T(8,128)}, f32[32,3,384]{2,0,1:T(8,128)S(1)}, u32[]{:S(2)}) copy-start(f32[32,3,384]{2,0,1:T(8,128)S(1)} %slice_multiply_fusion) | copy-start | bytes 442372
Sparse Core Ops, SparseCore 0:
  218.4 144.3 reduce-scatter.1
